TPU v7x, 256 devices: a whole 4x4x8 slice. The times are simulated.
256 devices in a mesh: expert: 16 (over y_lo, x, core), dp: 16 (over y_hi, z).
Axes of the slice: x: 4, y: 4 (y_hi: 2, y_lo: 2; y = y_hi * 2 + y_lo), z: 8, core: 2. Of those that a mesh axis runs over, the one named last changes fastest.
Arguments:
- attn_input: bfloat16 [12288, 4096], P('dp'), may hold values from -6 to 6
- query_grad: bfloat16 [12288, 8192], P('dp', 'expert'), may hold values from -6 to 6
- query_weight: float32 [8192, 4096], P(('expert', 'dp')), may hold values from -40 to 40
- moe_cotangent: bfloat16 [2048, 4096], P('expert', 'dp'), may hold values from -6 to 6
- expert_ids: int32 [2048, 8], P('expert'), may hold values from 0 to 31, all different within a row; in each aligned block of 128 rows (0 to 127, 128 to 255, ...) at most 40 rows name the same one
- route_weights: float32 [2048, 8], P('expert'), may hold values from 0.2 to 1
- gate_saved: bfloat16 [640, 32, 1536], P('dp', 'expert'), may hold values from -6 to 6
- up_saved: bfloat16 [640, 32, 1536], P('dp', 'expert'), may hold values from -6 to 6
- gate_weight: bfloat16 [32, 4096, 1536], P('expert', 'dp'), may hold values from -0.09375 to 0.09375
- up_weight: bfloat16 [32, 4096, 1536], P('expert', 'dp'), may hold values from -0.09375 to 0.09375
- down_weight: bfloat16 [32, 1536, 4096], P('expert', None, 'dp'), may hold values from -0.15625 to 0.15625
Outputs:
- query_weight_next: float32 [8192, 4096], P(('expert', 'dp'))
- moe_input_grad: float32 [2048, 4096], P('expert', 'dp')
Inputs may be any that keep to these rules, and one draw needn't show every extreme that they name: `expert_ids`: in each aligned block of 128 rows no expert is named by more than 40 rows, and one expert by exactly 40 rows in some block; each row names 8 different experts.
All inputs are finite; a program needn't handle non-finite values.
Results may differ from a plain program's by a relative error of at most 0.022.
Values may be sent and summed in bfloat16 or wider, within the bound.
A program may use at most 128 MiB of HBM per device.

v0:
```python
import jax
import jax.numpy as jnp
from jax import lax
from jax.sharding import PartitionSpec as P

step_rate = 0.01
epsilon = 1e-06


def slot_tables(expert_ids, route_weights, experts, capacity):
    expert_iota = lax.broadcasted_iota(jnp.int32, (1, 1, experts), 2)
    chosen = (expert_ids[:, :, None] == expert_iota).astype(jnp.int32)
    counts = jnp.sum(chosen, axis=1, dtype=jnp.int32)
    rows = counts.shape[0]
    earlier = lax.broadcasted_iota(jnp.int32, (rows, rows), 1) < lax.broadcasted_iota(
        jnp.int32, (rows, rows), 0
    )
    before = jnp.dot(
        earlier.astype(jnp.bfloat16),
        counts.astype(jnp.bfloat16),
        preferred_element_type=jnp.float32,
    ).astype(jnp.int32)
    position = jnp.sum(chosen * before[:, None, :], axis=2, dtype=jnp.int32)
    slot_code = position * experts + expert_ids
    slot_iota = lax.broadcasted_iota(jnp.int32, (1, 1, capacity * experts), 2)
    matched = slot_code[:, :, None] == slot_iota
    select = jnp.sum(matched.astype(jnp.float32), axis=1)
    scaled = jnp.sum(jnp.where(matched, route_weights[:, :, None], 0.0), axis=1)
    return (select, scaled)


def activation_grads(hidden, gate_vals, up_vals):
    gate_float = gate_vals.astype(jnp.float32)
    up_float = up_vals.astype(jnp.float32)
    sigmoid_vals = jax.nn.sigmoid(gate_float)
    gate_grad = hidden * up_float * sigmoid_vals * (1.0 + gate_float * (1.0 - sigmoid_vals))
    up_grad = hidden * gate_float * sigmoid_vals
    return jnp.stack([gate_grad, up_grad], axis=2).astype(jnp.bfloat16)


def weight_update(attn_input, query_grad, query_weight):
    gradient = lax.psum_scatter(
        lax.dot_general(
            query_grad, attn_input, (((0,), (0,)), ((), ())), preferred_element_type=jnp.float32
        ).astype(jnp.bfloat16),
        "dp",
        scatter_dimension=0,
        tiled=True,
    ).astype(jnp.float32)
    radial = jnp.mean(query_weight * gradient, axis=1, keepdims=True) / (
        jnp.mean(query_weight * query_weight, axis=1, keepdims=True) + epsilon
    )
    stepped = query_weight - step_rate * (gradient - radial * query_weight)
    return stepped * lax.rsqrt(jnp.mean(stepped * stepped, axis=1, keepdims=True) + epsilon)


def expert_update(
    moe_cotangent,
    expert_ids,
    route_weights,
    gate_saved,
    up_saved,
    gate_weight,
    up_weight,
    down_weight,
):
    groups = lax.axis_size("expert")
    experts = gate_weight.shape[0] * groups
    capacity = gate_saved.shape[0] * lax.axis_size("dp") // groups
    select, scaled = slot_tables(expert_ids, route_weights, experts, capacity)
    outgoing = jnp.dot(
        scaled.T,
        moe_cotangent.astype(jnp.float32),
        precision=lax.Precision.HIGHEST,
        preferred_element_type=jnp.float32,
    )
    outgoing = outgoing.astype(jnp.bfloat16).reshape(capacity, experts, moe_cotangent.shape[1])
    arrived = lax.all_to_all(outgoing, "expert", split_axis=1, concat_axis=0, tiled=True)
    hidden = lax.psum_scatter(
        jnp.einsum("sec,ehc->seh", arrived, down_weight, preferred_element_type=jnp.float32).astype(
            jnp.bfloat16
        ),
        "dp",
        scatter_dimension=0,
        tiled=True,
    ).astype(jnp.float32)
    grads_pair = activation_grads(hidden, gate_saved, up_saved)
    part_rows = lax.all_gather(grads_pair, "dp", axis=0, tiled=True)
    total = jnp.einsum(
        "seh,ech->sec", part_rows[:, :, 0], gate_weight, preferred_element_type=jnp.float32
    )
    total = total + jnp.einsum(
        "seh,ech->sec", part_rows[:, :, 1], up_weight, preferred_element_type=jnp.float32
    )
    slot_input = total.astype(jnp.bfloat16)
    returned_rows = lax.all_to_all(slot_input, "expert", split_axis=0, concat_axis=1, tiled=True)
    flat_rows = returned_rows.reshape(capacity * experts, returned_rows.shape[2])
    return jnp.dot(select.astype(jnp.bfloat16), flat_rows, preferred_element_type=jnp.float32)


def shards(
    attn_input,
    query_grad,
    query_weight,
    moe_cotangent,
    expert_ids,
    route_weights,
    gate_saved,
    up_saved,
    gate_weight,
    up_weight,
    down_weight,
):
    moe_input_grad = expert_update(
        moe_cotangent,
        expert_ids,
        route_weights,
        gate_saved,
        up_saved,
        gate_weight,
        up_weight,
        down_weight,
    )
    query_weight_next = weight_update(attn_input, query_grad, query_weight)
    return (query_weight_next, moe_input_grad)


def solution(mesh):
    placed = (
        P("dp", None),
        P("dp", "expert"),
        P(("expert", "dp"), None),
        P("expert", "dp"),
        P("expert", None),
        P("expert", None),
        P("dp", "expert", None),
        P("dp", "expert", None),
        P("expert", "dp", None),
        P("expert", "dp", None),
        P("expert", None, "dp"),
    )
    return jax.shard_map(
        shards,
        mesh=mesh,
        in_specs=placed,
        out_specs=(P(("expert", "dp"), None), P("expert", "dp")),
        check_vma=False,
    )
```

profile of v0, /device:TPU:1, one launch (start us, length us, event | category | flops | bytes accessed | tf_op | source)
XLA Modules:
  0.0 630.1 jit_solution(1963007149182575208)
XLA Ops:
  7.2 0.0 copy-start
  7.2 0.0 reduce-scatter.7.cloned.1.call-start
  7.2 0.8 convert_reduce_fusion.1
  8.0 0.1 convolution_convert_fusion.3
  8.2 0.7 select_reduce_fusion.1
  8.9 0.7 multiply_add_fusion
  9.6 0.1 copy.38
  9.7 0.8 copy.39
  10.5 4.1 convert_reduce_fusion
  14.6 1.6 convolution_convert_fusion.2
  16.2 0.4 copy.40
  16.6 18.3 %all_to_all.33 = bf16[40,32,256]{2,0,1:T(8,128)(2,1)S(1)} all-to-all(bf16[40,32,256]{2,0,1:T(8,128)(2,1)S(1)} %copy.40), channel_id=1, replica_groups=mesh['expert'=16,'dp'=16] {'expert'}, dimensions={1} | all-to-all | bytes 1310720 | tf_op jit(solution)/shard_map/all_to_all | solution.py:78
  35.0 0.0 copy-done
  35.0 1.2 fusion.2
  36.2 2.5 copy.49
  38.7 0.0 copy-start.6
  38.7 0.0 reduce-scatter.7.cloned.1.call-update
  38.7 0.0 reduce-scatter.5.cloned.1.call-start
  38.7 1.1 copy-done.6
  39.8 7.8 %convolution_convert_fusion = bf16[512,4096]{1,0:T(8,128)(2,1)} fusion(bf16[768,512]{1,0:T(8,128)(2,1)S(1)} %copy-done.6, bf16[768,4096]{1,0:T(8,128)(2,1)} %param.11), kind=kOutput, calls=%fused_computation | convolution fusion | flops 3223322624 | bytes 11272192 | tf_op jit(solution)/shard_map/dot_general | solution.py:43
  47.6 0.0 copy-start.3
  47.6 0.0 copy-start.4
  47.6 0.0 copy-start.1
  47.6 0.0 reduce-scatter.5.cloned.1.call-update
  47.6 0.0 all-gather.2.cloned.1.call-start
  47.6 200.5 %reduce-scatter.7.cloned.1.call-done = bf16[40,3072]{1,0:T(8,128)(2,1)} async-done(((bf16[640,3072]{1,0:T(8,128)(2,1)}), bf16[40,3072]{1,0:T(8,128)(2,1)}) %reduce-scatter.7.cloned.1.call-update) | async-done | bytes 245776
  248.1 0.0 copy-done.3
  248.1 0.0 copy-done.4
  248.1 1.2 fusion.22
  249.3 0.8 pad_maximum_fusion
  250.1 0.0 all-gather.2.cloned.1.call-update
  250.2 208.7 %reduce-scatter.5.cloned.1.call-done = bf16[32,4096]{1,0:T(8,128)(2,1)} async-done(((bf16[512,4096]{1,0:T(8,128)(2,1)}), bf16[32,4096]{1,0:T(8,128)(2,1)}) %reduce-scatter.5.cloned.1.call-update) | async-done | bytes 262160 | tf_op jit(solution)/shard_map/reduce_scatter | solution.py:42
  458.8 0.0 copy-done.1
  458.8 1.1 fusion.6
  460.0 1.3 multiply_reduce_fusion
  461.3 133.7 %all-gather.2.cloned.1.call-done = bf16[640,2,2,1536]{3,0,1,2:T(8,128)(2,1)} async-done(((bf16[40,2,2,1536]{3,0,1,2:T(8,128)(2,1)}), bf16[640,2,2,1536]{3,0,1,2:T(8,128)(2,1)}) %all-gather.2.cloned.1.call-update) | async-done | bytes 7864336 | tf_op jit(solution)/shard_map/all_gather | solution.py:88
  594.9 0.0 copy-start.5
  594.9 3.9 fusion
  598.9 0.9 copy-done.5
  599.8 2.7 fusion.5
  602.5 1.5 copy.44
  604.0 5.4 all-to-all-start.1
  609.3 0.0 copy-done.2
  609.3 1.0 fusion.20
  610.3 10.4 %all-to-all-done.1 = bf16[640,2,256]{2,1,0:T(2,128)(2,1)S(1)} async-done(((bf16[640,2,256]{2,1,0:T(2,128)(2,1)}), bf16[640,2,256]{2,1,0:T(2,128)(2,1)S(1)}, u32[]{:S(2)}, u32[]{:S(2)}) %all-to-all-start.1) | async-done | bytes 655392 | tf_op jit(solution)/shard_map/all_to_all | solution.py:96
  620.8 0.7 copy.58
  621.5 0.3 reshape.36
  621.7 1.9 fusion.24
  (4 shorter events, 0.1 us)
Async XLA Ops:
  7.2 27.8 %copy-start = (bf16[2,1536,256]{2,1,0:T(8,128)(2,1)S(1)}, bf16[2,1536,256]{2,1,0:T(8,128)(2,1)}, u32[]{:S(2)}) copy-start(bf16[2,1536,256]{2,1,0:T(8,128)(2,1)} %param.21) | copy-start | bytes 4718596
  7.2 240.9 %reduce-scatter.7.cloned.1.call-start = ((), (), s32[]{:S(2)}) async-start(), calls=%async_computation.6 | async-start | bytes 4177920
  38.7 1.1 copy-start.6
  38.7 420.2 %reduce-scatter.5.cloned.1.call-start = ((), (), s32[]{:S(2)}) async-start(), calls=%async_computation.4 | async-start | bytes 4456448 | tf_op jit(solution)/shard_map/reduce_scatter | solution.py:42
  47.6 200.5 %copy-start.3 = (bf16[40,2,1536]{2,1,0:T(2,128)(2,1)S(1)}, bf16[40,2,1536]{2,1,0:T(2,128)(2,1)}, u32[]{:S(2)}) copy-start(bf16[40,2,1536]{2,1,0:T(2,128)(2,1)} %param.18) | copy-start | bytes 737284
  47.6 200.5 %copy-start.4 = (bf16[40,2,1536]{2,1,0:T(2,128)(2,1)S(1)}, bf16[40,2,1536]{2,1,0:T(2,128)(2,1)}, u32[]{:S(2)}) copy-start(bf16[40,2,1536]{2,1,0:T(2,128)(2,1)} %param.17) | copy-start | bytes 737284
  47.6 411.3 %copy-start.1 = (f32[32,4096]{1,0:T(8,128)S(1)}, f32[32,4096]{1,0:T(8,128)}, u32[]{:S(2)}) copy-start(f32[32,4096]{1,0:T(8,128)} %param.13) | copy-start | bytes 1572868
  47.6 547.3 %all-gather.2.cloned.1.call-start = ((), (), s32[]{:S(2)}) async-start(), calls=%async_computation.5 | async-start | bytes 8355840 | tf_op jit(solution)/shard_map/all_gather | solution.py:88
  594.9 4.9 copy-start.5
  599.8 9.6 %copy-start.2 = (bf16[32,4096]{1,0:T(8,128)(2,1)S(1)}, bf16[32,4096]{1,0:T(8,128)(2,1)}, u32[]{:S(2)}) copy-start(bf16[32,4096]{1,0:T(8,128)(2,1)} %reduce-scatter.5.cloned.1.call-done) | copy-start | bytes 786436
  604.0 16.8 %all-to-all-start.1 = ((bf16[640,2,256]{2,1,0:T(2,128)(2,1)}), bf16[640,2,256]{2,1,0:T(2,128)(2,1)S(1)}, u32[]{:S(2)}, u32[]{:S(2)}) async-start(bf16[640,2,256]{2,1,0:T(2,128)(2,1)} %copy.44), calls=%async_computation.2 | async-start | bytes 1310720 | tf_op jit(solution)/shard_map/all_to_all | solution.py:96
Sparse Core Ops, SparseCore 0:
  38.8 209.2 reduce-scatter.6
  252.6 206.1 reduce-scatter.4
  462.0 132.8 all-gather.1
where the time goes:
time: 631 us; the launch traced here: 630 us
  waiting for transfers between devices  553 us (88%)
  matrix products  19.2 us (3%)
  blocking collectives  18.3 us (3%)
  between operations  13.8 us (2%)
  other arithmetic  11.8 us (2%)
  local copies, waits for them, and re-layouts  8.22 us (1%)
    reduce_scatter x1, waiting for transfers between devices, weight_update(): lax.psum_scatter(lax.dot_general(query_grad, attn_input, (((0,), (0,)), (...  209 us
    unnamed x4, waiting for transfers between devices  201 us
    all_gather x1, waiting for transfers between devices, expert_update(): part_rows = lax.all_gather(grads_pair, 'dp', axis=0, tiled=True)  134 us
    all_to_all x1, blocking collectives, expert_update(): lax.all_to_all(outgoing, 'expert', split_axis=1, concat_axis=0, tiled=True)  18.3 us
  transfers between devices with their start and end apart: 4, of which 4 were waited for; matrix products, arithmetic and copies ran while one was open for 2% of the time, Pallas kernels for 0%

commit v1 on v0

--- a/solution.py
+++ b/solution.py
@@ -5,6 +5,11 @@
 
 step_rate = 0.01
 epsilon = 1e-06
+
+
+def swapped_in(x, name, dim):
+    repeated = jnp.stack([x] * lax.axis_size(name))
+    return jnp.concatenate(lax.all_to_all(repeated, name, 0, 0), axis=dim)
 
 
 def slot_tables(expert_ids, route_weights, experts, capacity):
@@ -85,7 +90,7 @@
         tiled=True,
     ).astype(jnp.float32)
     grads_pair = activation_grads(hidden, gate_saved, up_saved)
-    part_rows = lax.all_gather(grads_pair, "dp", axis=0, tiled=True)
+    part_rows = swapped_in(grads_pair, "dp", 0)
     total = jnp.einsum(
         "seh,ech->sec", part_rows[:, :, 0], gate_weight, preferred_element_type=jnp.float32
     )

time: 631 us -> 600 us (0.951)
  waiting for transfers between devices: 553 us -> 508 us
  starting transfers between devices: 5.5 us -> 15.7 us
    all_gather x1 -> x0, waiting for transfers between devices: 134 us -> none  [expert_update(): part_rows = lax.all_gather(grads_pair, 'dp', axis=0, tiled=True)]
    reduce_scatter x1, waiting for transfers between devices: 209 us -> 290 us  [weight_update(): lax.psum_scatter(lax.dot_general(query_grad, attn_input, (((0,), (0,)), (...]
    unnamed x4 -> x3, waiting for transfers between devices: 201 us -> 209 us
  transfers between devices with their start and end apart: 4 -> 4, of which waited for: 4 -> 3; matrix products, arithmetic and copies ran while one was open for 2% -> 2% of each run, Pallas kernels for 0% -> 0%
where the time goes in v1:
time: 600 us; the launch traced here: 599 us
  waiting for transfers between devices  508 us (85%)
  blocking collectives  18.3 us (3%)
  matrix products  16.6 us (3%)
  starting transfers between devices  15.7 us (3%)
  local copies, waits for them, and re-layouts  14.2 us (2%)
  between operations  14.2 us (2%)
  other arithmetic  12 us (2%)
    reduce_scatter x1, waiting for transfers between devices, weight_update(): lax.psum_scatter(lax.dot_general(query_grad, attn_input, (((0,), (0,)), (...  290 us
    unnamed x3, waiting for transfers between devices  209 us
    all_to_all x1, blocking collectives, expert_update(): lax.all_to_all(outgoing, 'expert', split_axis=1, concat_axis=0, tiled=True)  18.3 us
  transfers between devices with their start and end apart: 4, of which 3 were waited for; matrix products, arithmetic and copies ran while one was open for 2% of the time, Pallas kernels for 0%

profile of v1, /device:TPU:1, one launch (start us, length us, event | category | flops | bytes accessed | tf_op | source)
XLA Modules:
  0.0 599.5 jit_solution(9703269155314856137)
XLA Ops:
  7.2 0.0 copy-start
  7.2 0.0 reduce-scatter.7.cloned.1.call-start
  7.2 0.8 convert_reduce_fusion.1
  8.0 0.1 convolution_convert_fusion.3
  8.2 0.7 select_reduce_fusion.1
  8.9 0.7 multiply_add_fusion
  9.6 0.1 copy.39
  9.7 0.8 copy.40
  10.5 4.1 convert_reduce_fusion
  14.6 1.6 convolution_convert_fusion.2
  16.2 0.4 copy.41
  16.6 18.3 %all_to_all.38 = bf16[40,32,256]{2,0,1:T(8,128)(2,1)S(1)} all-to-all(bf16[40,32,256]{2,0,1:T(8,128)(2,1)S(1)} %copy.41), channel_id=1, replica_groups=mesh['expert'=16,'dp'=16] {'expert'}, dimensions={1} | all-to-all | bytes 1310720 | tf_op jit(solution)/shard_map/all_to_all | solution.py:83
  35.0 0.0 copy-done
  35.0 1.2 fusion.2
  36.2 2.5 copy.51
  38.7 0.0 copy-start.3
  38.7 0.0 reduce-scatter.7.cloned.1.call-update
  38.7 209.4 %reduce-scatter.7.cloned.1.call-done = bf16[40,3072]{1,0:T(8,128)(2,1)} async-done(((bf16[640,3072]{1,0:T(8,128)(2,1)}), bf16[40,3072]{1,0:T(8,128)(2,1)}) %reduce-scatter.7.cloned.1.call-update) | async-done | bytes 245776
  248.1 0.0 copy-done.3
  248.1 0.0 copy-done.4
  248.1 1.2 fusion.22
  249.4 4.1 stack.11
  253.5 0.0 copy-start.6
  253.5 6.1 %all-to-all-start.1 = ((bf16[16,40,2,2,1536]{4,1,2,3,0:T(8,128)(2,1)}), bf16[16,40,2,2,1536]{4,1,2,3,0:T(8,128)(2,1)}, u32[]{:S(2)}, u32[]{:S(2)}) async-start(bf16[16,40,2,2,1536]{4,1,2,3,0:T(8,128)(2,1)} %stack.11), calls=%async_computation.2 | async-start | bytes 15728640 | tf_op jit(solution)/shard_map/all_to_all | solution.py:12
  259.5 0.0 reduce-scatter.5.cloned.1.call-start
  259.6 0.0 copy-done.6
  259.6 7.8 %convolution_convert_fusion = bf16[512,4096]{1,0:T(8,128)(2,1)} fusion(bf16[768,512]{1,0:T(8,128)(2,1)S(1)} %copy-done.6, bf16[768,4096]{1,0:T(8,128)(2,1)} %param.11), kind=kOutput, calls=%fused_computation | convolution fusion | flops 3223322624 | bytes 11272192 | tf_op jit(solution)/shard_map/dot_general | solution.py:48
  267.5 0.0 copy-start.1
  267.5 0.0 reduce-scatter.5.cloned.1.call-update
  267.5 289.6 %reduce-scatter.5.cloned.1.call-done = bf16[32,4096]{1,0:T(8,128)(2,1)} async-done(((bf16[512,4096]{1,0:T(8,128)(2,1)}), bf16[32,4096]{1,0:T(8,128)(2,1)}) %reduce-scatter.5.cloned.1.call-update) | async-done | bytes 262160 | tf_op jit(solution)/shard_map/reduce_scatter | solution.py:47
  557.1 0.0 copy-done.1
  557.1 1.1 fusion.6
  558.2 1.3 multiply_reduce_fusion
  559.5 0.0 all-to-all-done.1
  559.5 3.9 copy.45
  563.4 0.0 copy-start.5
  563.4 2.7 fusion
  566.1 0.0 copy-done.5
  566.1 0.0 copy-start.2
  566.1 1.2 fusion.5
  567.3 1.5 copy.46
  568.9 9.5 %all-to-all-start.2 = ((bf16[640,2,256]{2,1,0:T(2,128)(2,1)}), bf16[640,2,256]{2,1,0:T(2,128)(2,1)S(1)}, u32[]{:S(2)}, u32[]{:S(2)}) async-start(bf16[640,2,256]{2,1,0:T(2,128)(2,1)} %copy.46), calls=%async_computation.3 | async-start | bytes 1310720 | tf_op jit(solution)/shard_map/all_to_all | solution.py:101
  578.4 0.0 copy-done.2
  578.4 2.0 fusion.20
  580.4 9.4 %all-to-all-done.2 = bf16[640,2,256]{2,1,0:T(2,128)(2,1)S(1)} async-done(((bf16[640,2,256]{2,1,0:T(2,128)(2,1)}), bf16[640,2,256]{2,1,0:T(2,128)(2,1)S(1)}, u32[]{:S(2)}, u32[]{:S(2)}) %all-to-all-start.2) | async-done | bytes 655392 | tf_op jit(solution)/shard_map/all_to_all | solution.py:101
  589.8 0.7 copy.60
  590.5 0.3 reshape.51
  590.7 1.9 fusion.24
  (5 shorter events, 0.1 us)
Async XLA Ops:
  7.2 27.8 %copy-start = (bf16[2,1536,256]{2,1,0:T(8,128)(2,1)S(1)}, bf16[2,1536,256]{2,1,0:T(8,128)(2,1)}, u32[]{:S(2)}) copy-start(bf16[2,1536,256]{2,1,0:T(8,128)(2,1)} %param.21) | copy-start | bytes 4718596
  7.2 240.9 %reduce-scatter.7.cloned.1.call-start = ((), (), s32[]{:S(2)}) async-start(), calls=%async_computation.6 | async-start | bytes 4177920
  38.7 209.4 %copy-start.3 = (bf16[40,2,1536]{2,1,0:T(2,128)(2,1)S(1)}, bf16[40,2,1536]{2,1,0:T(2,128)(2,1)}, u32[]{:S(2)}) copy-start(bf16[40,2,1536]{2,1,0:T(2,128)(2,1)} %param.18) | copy-start | bytes 737284
  38.7 209.4 %copy-start.4 = (bf16[40,2,1536]{2,1,0:T(2,128)(2,1)S(1)}, bf16[40,2,1536]{2,1,0:T(2,128)(2,1)}, u32[]{:S(2)}) copy-start(bf16[40,2,1536]{2,1,0:T(2,128)(2,1)} %param.17) | copy-start | bytes 737284
  253.5 6.1 %copy-start.6 = (bf16[768,512]{1,0:T(8,128)(2,1)S(1)}, bf16[768,512]{1,0:T(8,128)(2,1)}, u32[]{:S(2)}) copy-start(bf16[768,512]{1,0:T(8,128)(2,1)} %param.12) | copy-start | bytes 2359300
  253.5 306.0 %all-to-all-start.1 = ((bf16[16,40,2,2,1536]{4,1,2,3,0:T(8,128)(2,1)}), bf16[16,40,2,2,1536]{4,1,2,3,0:T(8,128)(2,1)}, u32[]{:S(2)}, u32[]{:S(2)}) async-start(bf16[16,40,2,2,1536]{4,1,2,3,0:T(8,128)(2,1)} %stack.11), calls=%async_computation.2 | async-start | bytes 15728640 | tf_op jit(solution)/shard_map/all_to_all | solution.py:12
  259.5 297.5 %reduce-scatter.5.cloned.1.call-start = ((), (), s32[]{:S(2)}) async-start(), calls=%async_computation.5 | async-start | bytes 4456448 | tf_op jit(solution)/shard_map/reduce_scatter | solution.py:47
  267.5 289.6 %copy-start.1 = (f32[32,4096]{1,0:T(8,128)S(1)}, f32[32,4096]{1,0:T(8,128)}, u32[]{:S(2)}) copy-start(f32[32,4096]{1,0:T(8,128)} %param.13) | copy-start | bytes 1572868
  563.4 2.8 copy-start.5
  566.1 12.3 %copy-start.2 = (bf16[32,4096]{1,0:T(8,128)(2,1)S(1)}, bf16[32,4096]{1,0:T(8,128)(2,1)}, u32[]{:S(2)}) copy-start(bf16[32,4096]{1,0:T(8,128)(2,1)} %reduce-scatter.5.cloned.1.call-done) | copy-start | bytes 786436
  568.9 20.9 %all-to-all-start.2 = ((bf16[640,2,256]{2,1,0:T(2,128)(2,1)}), bf16[640,2,256]{2,1,0:T(2,128)(2,1)S(1)}, u32[]{:S(2)}, u32[]{:S(2)}) async-start(bf16[640,2,256]{2,1,0:T(2,128)(2,1)} %copy.46), calls=%async_computation.3 | async-start | bytes 1310720 | tf_op jit(solution)/shard_map/all_to_all | solution.py:101
Sparse Core Ops, SparseCore 0:
  38.8 209.2 reduce-scatter.6
  267.6 289.4 reduce-scatter.4
